TPU v7x, 256 devices: a whole 4x4x8 slice. The times are simulated.
256 devices in a mesh: seq: 16 (over z, core), dp: 16 (over y, x).
Axes of the slice: x: 4, y: 4, z: 8, core: 2. Of those that a mesh axis runs over, the one named last changes fastest.
Arguments:
- queries: bfloat16 [16, 2048, 1280], P('dp', 'seq'), may hold values from -43 to 43
- key_rows: bfloat16 [16, 2048, 1280], P('dp', 'seq'), may hold values from -7 to 7
- value_rows: bfloat16 [16, 2048, 1280], P('dp', 'seq'), may hold values from -6 to 6
- resid_in: bfloat16 [16, 2048, 1280], P('dp', 'seq'), may hold values from -6 to 6
- llm_grad: bfloat16 [16, 3072, 1280], P('dp', 'seq'), may hold values from -6 to 6
- vision_slot: int32 [16, 3072], P('dp', 'seq'), may hold values from -1 to 2047, as said below
- window_mask: int32 [16, 32, 2], P('dp', 'seq'), may hold values from 0 to 1, as said below
- w_up: bfloat16 [1280, 2560], P('dp'), may hold values from -0.15625 to 0.15625
- w_down: bfloat16 [2560, 1280], P('dp'), may hold values from -0.125 to 0.125
- norm_gain: bfloat16 [1280], P('dp'), may hold values from 0.25 to 1.75
Outputs:
- grad_query: bfloat16 [16, 2048, 1280], P('dp', 'seq')
- grad_key: bfloat16 [16, 2048, 1280], P('dp', 'seq')
- grad_value: bfloat16 [16, 2048, 1280], P('dp', 'seq')
- grad_resid: bfloat16 [16, 2048, 1280], P('dp', 'seq')
- grad_up: bfloat16 [1280, 2560], P('seq', 'dp')
- grad_down: bfloat16 [2560, 1280], P('seq', 'dp')
- grad_gain: float32 [1280], replicated
Inputs may be any that keep to these rules, and one draw needn't show every extreme that they name: `vision_slot`: -1 marks a text position; every vision token of a batch stands at exactly one position. Positions come in aligned runs of 16: each run is text or the 16 consecutive vision tokens of one tile, in order. Each language-model shard holds exactly 8 tiles, and at most 32 vision tokens of one owner; in every batch, for every owner, some shard holds exactly 32 of that owner's vision tokens. `window_mask`: each owner's 2 blocks are split into images of one or more consecutive blocks; a block attends to exactly the blocks of its own image, itself included (entry i % 2 of row i is 1).
All inputs are finite; a program needn't handle non-finite values.
Results may differ from a plain program's by a relative error of at most 0.023.
Values may be sent and summed in bfloat16 or wider, within the bound.
A program may use at most 128 MiB of HBM per device.

v0:
```python
import math
import jax
import jax.numpy as jnp
from jax import lax
from jax.sharding import PartitionSpec as P

HEADS = 16
HDIM = 80
BLK = 64
PIECE = 16


def contract(left, right, left_dim, right_dim):
    return lax.dot_general(
        left, right, (((left_dim,), (right_dim,)), ((), ())), preferred_element_type=jnp.float32
    )


def per_device(
    queries,
    key_rows,
    value_rows,
    resid_in,
    llm_grad,
    vision_slot,
    window_mask,
    w_up,
    w_down,
    norm_gain,
):
    seq_count = lax.axis_size("seq")
    data_count = lax.axis_size("dp")
    query = queries[0]
    key_block = key_rows[0]
    value_block = value_rows[0]
    tokens, feat_dim = query.shape
    att_scale = 1.0 / math.sqrt(HDIM)
    up_full, down_full, gain_full = (
        lax.all_gather(w_up, "dp", axis=0, tiled=True),
        lax.all_gather(w_down, "dp", axis=0, tiled=True),
        lax.all_gather(norm_gain, "dp", axis=0, tiled=True),
    )
    slot_ids = vision_slot[0]
    piece_count = tokens // PIECE
    capacity = PIECE * (1 + (piece_count + seq_count - 2) // seq_count)
    owner_of = jnp.where(slot_ids >= 0, slot_ids // tokens, seq_count)
    onehot = (owner_of[:, None] == jnp.arange(seq_count)[None, :]).astype(jnp.int32)
    ranking = jnp.sum((jnp.cumsum(onehot, axis=0) - 1) * onehot, axis=1)
    target = jnp.where(slot_ids >= 0, owner_of * capacity + ranking, seq_count * capacity)
    send_rows = (
        jnp.zeros((seq_count * capacity, feat_dim), jnp.bfloat16)
        .at[target]
        .set(llm_grad[0], mode="drop")
    )
    send_ids = (
        jnp.full((seq_count * capacity,), -1, jnp.int32)
        .at[target]
        .set(jnp.where(slot_ids >= 0, slot_ids % tokens, -1), mode="drop")
    )
    recv_rows = lax.all_to_all(
        send_rows.reshape(seq_count, capacity, feat_dim),
        "seq",
        split_axis=0,
        concat_axis=0,
        tiled=True,
    )
    recv_ids = lax.all_to_all(
        send_ids.reshape(seq_count, capacity), "seq", split_axis=0, concat_axis=0, tiled=True
    )
    flat_ids = recv_ids.reshape(seq_count * capacity)
    landing = jnp.where(flat_ids >= 0, flat_ids, tokens)
    grad_rows = (
        jnp.zeros((tokens, feat_dim), jnp.bfloat16)
        .at[landing]
        .set(recv_rows.reshape(seq_count * capacity, feat_dim), mode="drop")
    )
    allowed = jnp.repeat(jnp.repeat(window_mask[0] > 0, BLK, axis=0), BLK, axis=1)
    q_heads = query.reshape(tokens, HEADS, HDIM)
    k_heads = key_block.reshape(tokens, HEADS, HDIM)
    v_heads = value_block.reshape(tokens, HEADS, HDIM)
    scores = (
        jnp.einsum("qhd,khd->hqk", q_heads, k_heads, preferred_element_type=jnp.float32) * att_scale
    )
    masked = jnp.where(allowed[None], scores, -jnp.inf)
    highest = jnp.max(masked, axis=2, keepdims=True)
    exp_terms = jnp.where(allowed[None], jnp.exp(masked - highest), 0.0)
    attn_probs = exp_terms / jnp.sum(exp_terms, axis=2, keepdims=True)
    probs_low = attn_probs.astype(jnp.bfloat16)
    attn_heads = jnp.einsum(
        "hqk,khd->qhd", probs_low, v_heads, preferred_element_type=jnp.float32
    ).astype(jnp.bfloat16)
    attn_out = attn_heads.reshape(tokens, feat_dim)
    hidden = resid_in[0].astype(jnp.float32) + attn_out.astype(jnp.float32)
    center = jnp.mean(hidden, axis=1, keepdims=True)
    variance = jnp.mean(jnp.square(hidden - center), axis=1, keepdims=True)
    inverse = lax.rsqrt(variance + 1e-06)
    normal_unit = (hidden - center) * inverse
    gain_wide = gain_full.astype(jnp.float32)
    normed = (normal_unit * gain_wide).astype(jnp.bfloat16)
    pre_act = jnp.dot(normed, up_full, preferred_element_type=jnp.float32)
    sig_gate = jax.nn.sigmoid(1.702 * pre_act)
    act_low = (pre_act * sig_gate).astype(jnp.bfloat16)
    down_term = contract(act_low, grad_rows, 0, 0)
    d_act = contract(grad_rows, down_full, 1, 1)
    d_pre = (d_act * (sig_gate + 1.702 * pre_act * sig_gate * (1.0 - sig_gate))).astype(
        jnp.bfloat16
    )
    d_normed = contract(d_pre, up_full, 1, 1)
    gain_term = jnp.sum(d_normed * normal_unit, axis=0)
    d_unit = d_normed * gain_wide
    d_hidden = inverse * (
        d_unit
        - jnp.mean(d_unit, axis=1, keepdims=True)
        - normal_unit * jnp.mean(d_unit * normal_unit, axis=1, keepdims=True)
    )
    grad_resid = (grad_rows.astype(jnp.float32) + d_hidden).astype(jnp.bfloat16)
    up_term = contract(normed, d_pre, 0, 0)
    grad_heads = grad_resid.reshape(tokens, HEADS, HDIM)
    grad_value = jnp.einsum(
        "hqk,qhd->khd", probs_low, grad_heads, preferred_element_type=jnp.float32
    ).astype(jnp.bfloat16)
    d_probs = jnp.einsum("qhd,khd->hqk", grad_heads, v_heads, preferred_element_type=jnp.float32)
    delta = jnp.einsum("qhd,qhd->hq", grad_heads, attn_heads, preferred_element_type=jnp.float32)
    d_scores = (attn_probs * (d_probs - delta[:, :, None]) * att_scale).astype(jnp.bfloat16)
    grad_query = jnp.einsum(
        "hqk,khd->qhd", d_scores, k_heads, preferred_element_type=jnp.float32
    ).astype(jnp.bfloat16)
    grad_key = jnp.einsum(
        "hqk,qhd->khd", d_scores, q_heads, preferred_element_type=jnp.float32
    ).astype(jnp.bfloat16)
    up_part, down_part = (
        lax.psum_scatter(
            up_term.astype(jnp.bfloat16), "seq", scatter_dimension=0, tiled=True
        ).astype(jnp.float32),
        lax.psum_scatter(
            down_term.astype(jnp.bfloat16), "seq", scatter_dimension=0, tiled=True
        ).astype(jnp.float32),
    )
    up_panel, down_panel = (
        lax.psum_scatter(
            up_part.astype(jnp.bfloat16), "dp", scatter_dimension=1, tiled=True
        ).astype(jnp.float32),
        lax.psum_scatter(
            down_part.astype(jnp.bfloat16), "dp", scatter_dimension=1, tiled=True
        ).astype(jnp.float32),
    )
    factor = 1.0 / math.sqrt(data_count * seq_count * tokens)
    gain_total = lax.psum(gain_term, ("seq", "dp"))
    return (
        grad_query.reshape(1, tokens, feat_dim),
        grad_key.reshape(1, tokens, feat_dim),
        grad_value.reshape(1, tokens, feat_dim),
        grad_resid[None],
        (up_panel * factor).astype(jnp.bfloat16),
        (down_panel * factor).astype(jnp.bfloat16),
        gain_total * factor,
    )


def solution(mesh):
    in_specs = (
        P("dp", "seq", None),
        P("dp", "seq", None),
        P("dp", "seq", None),
        P("dp", "seq", None),
        P("dp", "seq", None),
        P("dp", "seq"),
        P("dp", "seq", None),
        P("dp", None),
        P("dp", None),
        P("dp"),
    )
    out_specs = (
        P("dp", "seq", None),
        P("dp", "seq", None),
        P("dp", "seq", None),
        P("dp", "seq", None),
        P("seq", "dp"),
        P("seq", "dp"),
        P(),
    )
    return jax.shard_map(
        per_device, mesh=mesh, in_specs=in_specs, out_specs=out_specs, check_vma=False
    )
```

profile of v0, /device:TPU:2, one launch (start us, length us, event | category | flops | bytes accessed | tf_op | source)
XLA Modules:
  0.0 466.7 jit_solution(10220901300629912734)
XLA Ops:
  7.2 0.7 all-gather.5.cloned.1.call-update
  8.0 0.7 all-gather.3.cloned.1.call-update
  8.7 0.7 fusion.20
  9.4 0.6 reduce-window.6
  10.3 0.7 compare_select_fusion.2
  11.0 1.2 scatter_custom_fusion
  12.2 0.7 all_to_all.9
  12.9 8.6 %all-to-all-start = ((s32[16,1,32]{2,1,0:T(1,128)}), s32[16,1,32]{2,1,0:T(1,128)S(1)}, u32[]{:S(2)}, u32[]{:S(2)}) async-start(s32[16,1,32]{2,1,0:T(1,128)} %all_to_all.9), calls=%async_computation | async-start | bytes 16384 | tf_op jit(solution)/shard_map/all_to_all | solution.py:67
  21.5 2.7 scatter_custom_fusion.1
  24.1 4.9 %all-to-all-done = s32[16,1,32]{2,1,0:T(1,128)S(1)} async-done(((s32[16,1,32]{2,1,0:T(1,128)}), s32[16,1,32]{2,1,0:T(1,128)S(1)}, u32[]{:S(2)}, u32[]{:S(2)}) %all-to-all-start) | async-done | bytes 2080 | tf_op jit(solution)/shard_map/all_to_all | solution.py:67
  29.0 3.8 all-to-all-start.1
  33.4 0.4 copy-done.10
  34.4 1.5 fusion.35
  35.9 1.6 convolution_convert_fusion.3
  37.5 0.7 copy-done.6
  38.5 0.3 copy-done.16
  38.9 0.6 dynamic-slice
  40.1 0.2 dynamic-update-slice
  40.4 37.7 %all-reduce.1 = bf16[1280]{0:T(1024)(128)(2,1)S(1)} all-reduce(bf16[1280]{0:T(1024)(128)(2,1)S(1)} %dynamic-update-slice), channel_id=1, replica_groups=mesh['seq'=16,'dp'=16] {'dp'}, use_global_device_ids=true, to_apply=%add.1 | all-reduce | flops 1280 | bytes 5120
  78.4 0.5 broadcast.297
  79.0 0.7 reduce.7
  79.7 2.9 scatter_custom_fusion.2
  82.7 3.9 fusion.31
  86.6 64.3 %all-gather.3.cloned.1.call-done = bf16[2560,1280]{1,0:T(8,128)(2,1)} async-done(((bf16[160,1280]{1,0:T(8,128)(2,1)}), bf16[2560,1280]{1,0:T(8,128)(2,1)}) %all-gather.3.cloned.1.call-update) | async-done | bytes 6553616 | tf_op jit(solution)/shard_map/all_gather | solution.py:40
  151.0 5.1 %fusion.1 = bf16[128,2560]{1,0:T(8,128)(2,1)S(1)} fusion(bf16[128,1280]{1,0:T(8,128)(2,1)S(1)} %scatter_custom_fusion.2, bf16[2560,1280]{1,0:T(8,128)(2,1)} %all-gather.3.cloned.1.call-done, f32[128,2560]{1,0:T(8,128)S(1)} %fusion.31), kind=kOutput, calls=%fused_computation.7 | convolution fusion | flops 842137600 | bytes 8847360 | tf_op jit(solution)/shard_map/dot_general | solution.py:14
  156.1 4.7 convolution_convert_fusion.1
  160.8 4.6 convolution_convert_fusion
  165.5 5.2 %multiply_reduce_fusion = (f32[1280]{0:T(1024)S(1)}, f32[128]{0:T(128)S(1)}, f32[128]{0:T(128)S(1)}, f32[128,1280]{1,0:T(8,128)S(1)}) fusion(f32[128,1280]{1,0:T(8,128)S(1)} %get-tuple-element.32, f32[128]{0:T(128)S(1)} %add_rsqrt_fusion, f32[128]{0:T(128)S(1)} %broadcast_multiply_fusion.3, f32[1280]{0:T(1024)S(1)} %convert_element_type.92, ...), kind=kOutput, calls=%fused_computation.26 | convolution fusion | flops 840169984 | bytes 8531968 | tf_op jit(solution)/shard_map/dot_general | solution.py:14
  170.7 57.6 %reduce-scatter.9.cloned.1.call-done = bf16[80,2560]{1,0:T(8,128)(2,1)} async-done(((bf16[1280,2560]{1,0:T(8,128)(2,1)}), bf16[80,2560]{1,0:T(8,128)(2,1)}) %reduce-scatter.9.cloned.1.call-update) | async-done | bytes 409616 | tf_op jit(solution)/shard_map/reduce_scatter | solution.py:132
  228.3 2.1 copy.80
  230.5 0.3 add_convert_fusion
  231.0 0.4 copy-done.7
  231.5 1.7 fusion.8
  233.2 0.3 convolution_convert_fusion.2
  233.6 63.2 %reduce-scatter.11.cloned.1.call-done = bf16[160,1280]{1,0:T(8,128)(2,1)} async-done(((bf16[2560,1280]{1,0:T(8,128)(2,1)}), bf16[160,1280]{1,0:T(8,128)(2,1)}) %reduce-scatter.11.cloned.1.call-update) | async-done | bytes 409616 | tf_op jit(solution)/shard_map/reduce_scatter | solution.py:135
  296.7 2.1 copy.82
  298.9 0.5 convolution_convert_fusion.5
  299.4 0.9 copy.64
  300.3 0.9 copy.65
  301.2 0.5 convolution_convert_fusion.4
  301.7 0.9 copy.66
  302.6 75.3 %psum.7 = f32[1280]{0:T(1024)S(1)} all-reduce(f32[1280]{0:T(1024)S(1)} %get-tuple-element.28), channel_id=1, replica_groups=mesh['seq'=16,'dp'=16] {'seq','dp'}, use_global_device_ids=true, to_apply=%region_17.18 | all-reduce | flops 1280 | bytes 10240 | tf_op jit(solution)/shard_map/psum | solution.py:148
  377.9 0.6 broadcast_multiply_fusion
  378.5 0.9 copy.81
  379.4 0.6 multiply_convert_fusion.4
  380.0 78.3 %reduce-scatter.15.cloned.1.call-done = bf16[80,160]{1,0:T(8,128)(2,1)} async-done(((bf16[1280,160]{1,0:T(8,128)(2,1)}), bf16[80,160]{1,0:T(8,128)(2,1)}) %reduce-scatter.15.cloned.1.call-update) | async-done | bytes 25616
  458.4 0.9 copy.83
  459.2 0.6 multiply_convert_fusion.3
  (73 shorter events, 2.8 us)
Async XLA Ops:
  7.2 14.3 %copy-start = (bf16[1,192,1280]{2,1,0:T(8,128)(2,1)S(1)}, bf16[1,192,1280]{2,1,0:T(8,128)(2,1)}, u32[]{:S(2)}) copy-start(bf16[1,192,1280]{2,1,0:T(8,128)(2,1)} %param.14) | copy-start | bytes 1474564
  7.2 75.5 %all-gather.5.cloned.1.call-start = ((), (), s32[]{:S(2)}) async-start(), calls=%async_computation.7 | async-start | bytes 6963200 | tf_op jit(solution)/shard_map/all_gather | solution.py:39
  7.9 143.1 %all-gather.3.cloned.1.call-start = ((), (), s32[]{:S(2)}) async-start(), calls=%async_computation.6 | async-start | bytes 6963200 | tf_op jit(solution)/shard_map/all_gather | solution.py:40
  12.9 16.1 %all-to-all-start = ((s32[16,1,32]{2,1,0:T(1,128)}), s32[16,1,32]{2,1,0:T(1,128)S(1)}, u32[]{:S(2)}, u32[]{:S(2)}) async-start(s32[16,1,32]{2,1,0:T(1,128)} %all_to_all.9), calls=%async_computation | async-start | bytes 16384 | tf_op jit(solution)/shard_map/all_to_all | solution.py:67
  29.0 3.9 copy-start.8
  29.0 4.1 copy-start.9
  29.0 50.7 %all-to-all-start.1 = ((bf16[16,32,1280]{2,1,0:T(8,128)(2,1)}), bf16[16,32,1280]{2,1,0:T(8,128)(2,1)S(1)}, u32[]{:S(2)}, u32[]{:S(2)}) async-start(bf16[16,32,1280]{2,1,0:T(8,128)(2,1)} %bitcast.13), calls=%async_computation.1 | async-start | bytes 2621440 | tf_op jit(solution)/shard_map/all_to_all | solution.py:60
  32.8 1.0 copy-start.10
  32.9 1.2 copy-start.14
  32.9 195.4 %reduce-scatter.9.cloned.1.call-start = ((), (), s32[]{:S(2)}) async-start(), calls=%async_computation.8 | async-start | bytes 6963200 | tf_op jit(solution)/shard_map/reduce_scatter | solution.py:132
  33.2 2.7 copy-start.3
  33.8 2.0 copy-start.11
  34.0 1.8 copy-start.1
  37.5 0.7 copy-start.6
  38.2 0.7 copy-start.16
  38.2 1.9 copy-start.15
  38.3 39.8 %copy-start.13 = (bf16[1,128,1280]{2,1,0:T(8,128)(2,1)S(1)}, bf16[1,128,1280]{2,1,0:T(8,128)(2,1)}, u32[]{:S(2)}) copy-start(bf16[1,128,1280]{2,1,0:T(8,128)(2,1)} %param.13) | copy-start | bytes 983044
  160.8 136.0 %reduce-scatter.11.cloned.1.call-start = ((), (), s32[]{:S(2)}) async-start(), calls=%async_computation.9 | async-start | bytes 6963200 | tf_op jit(solution)/shard_map/reduce_scatter | solution.py:135
  165.5 213.0 %reduce-scatter.13.cloned.1.call-start = ((), (), s32[]{:S(2)}) async-start(), calls=%async_computation.10 | async-start | bytes 696320
  230.4 228.0 %reduce-scatter.15.cloned.1.call-start = ((), (), s32[]{:S(2)}) async-start(), calls=%async_computation.11 | async-start | bytes 696320
  230.4 1.0 copy-start.7
  230.4 1.1 copy-start.12
  230.8 2.4 copy-start.5
  231.5 1.7 copy-start.4
  233.2 65.6 %copy-start.2 = (bf16[1,128,1280]{1,2,0:T(8,128)(2,1)S(1)}, bf16[1,128,1280]{1,2,0:T(8,128)(2,1)}, u32[]{:S(2)}) copy-start(bf16[1,128,1280]{1,2,0:T(8,128)(2,1)} %copy-done.1) | copy-start | bytes 983044
  298.9 2.3 copy-start.17
Sparse Core Ops, SparseCore 0:
  10.4 70.4 all-gather.4
  83.3 67.5 all-gather.2
  160.9 67.3 reduce-scatter.8
  230.7 65.9 reduce-scatter.10
  300.1 76.7 reduce-scatter.12
  380.2 78.0 reduce-scatter.14
where the time goes:
time: 467 us
  waiting for transfers between devices  270 us (58%)
  blocking collectives  113 us (24%)
  matrix products  29.6 us (6%)
  local copies, waits for them, and re-layouts  21.1 us (5%)
  between operations  15.1 us (3%)
  starting transfers between devices  12.6 us (3%)
  other arithmetic  5.58 us (1%)
    unnamed x8, waiting for transfers between devices  79.8 us
    psum x1, blocking collectives, per_device(): gain_total = lax.psum(gain_term, ('seq', 'dp'))  75.3 us
    all_gather x1, waiting for transfers between devices, per_device(): lax.all_gather(w_down, 'dp', axis=0, tiled=True)  64.3 us
    reduce_scatter x1, waiting for transfers between devices, per_device(): lax.psum_scatter(down_term.astype(jnp.bfloat16), 'seq', scatter_dimension...  63.2 us
    reduce_scatter x1, waiting for transfers between devices, per_device(): lax.psum_scatter(up_term.astype(jnp.bfloat16), 'seq', scatter_dimension=0...  57.6 us
    unnamed x1, blocking collectives  37.7 us
    dot_general x4, matrix products, contract(): lax.dot_general(left, right, (((left_dim,), (right_dim,)), ((), ())), pre...  19.6 us
    unnamed x49, local copies, waits for them, and re-layouts  12.1 us
  transfers between devices with their start and end apart: 8, of which 5 were waited for; matrix products, arithmetic and copies ran while one was open for 9% of the time, Pallas kernels for 0%

commit v1 on v0

--- a/solution.py
+++ b/solution.py
@@ -145,7 +145,7 @@
         ).astype(jnp.float32),
     )
     factor = 1.0 / math.sqrt(data_count * seq_count * tokens)
-    gain_total = lax.psum(gain_term, ("seq", "dp"))
+    gain_total = jnp.sum(lax.all_gather(gain_term, ("seq", "dp")), axis=0)
     return (
         grad_query.reshape(1, tokens, feat_dim),
         grad_key.reshape(1, tokens, feat_dim),

time: 467 us -> 574 us (1.23)
  waiting for transfers between devices: 270 us -> 448 us
  blocking collectives: 113 us -> 37.8 us
    all_gather x0 -> x1, waiting for transfers between devices: none -> 99.6 us  [per_device(): gain_total = jnp.sum(lax.all_gather(gain_term, ('seq', 'dp')), axis=0)]
    unnamed x8 -> x9, waiting for transfers between devices: 79.8 us -> 160 us
    psum x1 -> x0, blocking collectives: 75.3 us -> none  [per_device(): gain_total = lax.psum(gain_term, ('seq', 'dp'))]
    unnamed x49 -> x52, local copies, waits for them, and re-layouts: 12.1 us -> 14.1 us
  transfers between devices with their start and end apart: 8 -> 9, of which waited for: 5 -> 7; matrix products, arithmetic and copies ran while one was open for 9% -> 8% of each run, Pallas kernels for 0% -> 0%
where the time goes in v1:
time: 574 us; the launch traced here: 573 us
  waiting for transfers between devices  448 us (78%)
  blocking collectives  37.8 us (7%)
  matrix products  27.4 us (5%)
  local copies, waits for them, and re-layouts  23.8 us (4%)
  between operations  15.2 us (3%)
  starting transfers between devices  13.4 us (2%)
  other arithmetic  7.67 us (1%)
    unnamed x9, waiting for transfers between devices  160 us
    all_gather x1, waiting for transfers between devices, per_device(): gain_total = jnp.sum(lax.all_gather(gain_term, ('seq', 'dp')), axis=0)  99.6 us
    all_gather x1, waiting for transfers between devices, per_device(): lax.all_gather(w_down, 'dp', axis=0, tiled=True)  63.9 us
    reduce_scatter x1, waiting for transfers between devices, per_device(): lax.psum_scatter(down_term.astype(jnp.bfloat16), 'seq', scatter_dimension...  62.8 us
    reduce_scatter x1, waiting for transfers between devices, per_device(): lax.psum_scatter(up_term.astype(jnp.bfloat16), 'seq', scatter_dimension=0...  56.9 us
    unnamed x1, blocking collectives  37.8 us
    dot_general x4, matrix products, contract(): lax.dot_general(left, right, (((left_dim,), (right_dim,)), ((), ())), pre...  19.6 us
    unnamed x52, local copies, waits for them, and re-layouts  14.1 us
  transfers between devices with their start and end apart: 9, of which 7 were waited for; matrix products, arithmetic and copies ran while one was open for 8% of the time, Pallas kernels for 0%

profile of v1, /device:TPU:2, one launch (start us, length us, event | category | flops | bytes accessed | tf_op | source)
XLA Modules:
  0.0 573.0 jit_solution(10131701487325854210)
XLA Ops:
  7.2 0.7 all-gather.8.cloned.1.call-update
  8.0 0.7 all-gather.6.cloned.1.call-update
  8.7 0.7 fusion.20
  9.4 0.6 reduce-window.6
  10.3 0.7 compare_select_fusion.2
  11.0 1.2 scatter_custom_fusion
  12.2 0.7 all_to_all.9
  12.9 8.6 %all-to-all-start = ((s32[16,1,32]{2,1,0:T(1,128)}), s32[16,1,32]{2,1,0:T(1,128)S(1)}, u32[]{:S(2)}, u32[]{:S(2)}) async-start(s32[16,1,32]{2,1,0:T(1,128)} %all_to_all.9), calls=%async_computation | async-start | bytes 16384 | tf_op jit(solution)/shard_map/all_to_all | solution.py:67
  21.5 2.7 scatter_custom_fusion.1
  24.1 4.9 all-to-all-done
  29.0 4.5 all-to-all-start.1
  34.1 0.4 copy-done.10
  35.0 0.5 fusion.35
  35.6 0.9 copy-done.17
  36.9 0.7 copy-done.6
  38.3 0.6 dynamic-slice
  39.8 37.8 %all-reduce.1 = bf16[1280]{0:T(1024)(128)(2,1)S(1)} all-reduce(bf16[1280]{0:T(1024)(128)(2,1)S(1)} %dynamic-update-slice), channel_id=1, replica_groups=mesh['seq'=16,'dp'=16] {'dp'}, use_global_device_ids=true, to_apply=%add.1 | all-reduce | flops 1280 | bytes 5120
  78.1 0.5 broadcast.297
  78.6 0.7 reduce.8
  79.4 3.7 scatter_custom_fusion.2
  83.1 3.9 fusion.31
  87.0 63.9 %all-gather.6.cloned.1.call-done = bf16[2560,1280]{1,0:T(8,128)(2,1)} async-done(((bf16[160,1280]{1,0:T(8,128)(2,1)}), bf16[2560,1280]{1,0:T(8,128)(2,1)}) %all-gather.6.cloned.1.call-update) | async-done | bytes 6553616 | tf_op jit(solution)/shard_map/all_gather | solution.py:40
  151.0 5.1 fusion.1
  156.1 4.7 convolution_convert_fusion.1
  160.8 4.6 convolution_convert_fusion
  165.5 5.2 multiply_reduce_fusion
  170.7 0.6 reshape.270
  171.4 56.9 %reduce-scatter.9.cloned.1.call-done = bf16[80,2560]{1,0:T(8,128)(2,1)} async-done(((bf16[1280,2560]{1,0:T(8,128)(2,1)}), bf16[80,2560]{1,0:T(8,128)(2,1)}) %reduce-scatter.9.cloned.1.call-update) | async-done | bytes 409616 | tf_op jit(solution)/shard_map/reduce_scatter | solution.py:132
  228.3 2.1 copy.80
  231.1 0.4 copy-done.7
  231.5 0.4 copy-done.12
  232.0 1.7 fusion.8
  234.0 62.8 %reduce-scatter.11.cloned.1.call-done = bf16[160,1280]{1,0:T(8,128)(2,1)} async-done(((bf16[2560,1280]{1,0:T(8,128)(2,1)}), bf16[160,1280]{1,0:T(8,128)(2,1)}) %reduce-scatter.11.cloned.1.call-update) | async-done | bytes 409616 | tf_op jit(solution)/shard_map/reduce_scatter | solution.py:135
  296.7 2.1 copy.82
  298.9 0.5 convolution_convert_fusion.5
  299.4 0.9 copy.64
  300.3 0.9 copy.65
  301.2 0.5 convolution_convert_fusion.4
  301.7 0.9 copy.66
  302.6 99.6 %all-gather.10.cloned.1.call-done = f32[256,1,1280]{2,1,0:T(1,128)} async-done(((f32[1,1,1280]{2,1,0:T(1,128)}), f32[256,1,1280]{2,1,0:T(1,128)}) %all-gather.10.cloned.1.call-update) | async-done | bytes 1310736 | tf_op jit(solution)/shard_map/all_gather | solution.py:148
  402.2 2.1 reduce_sum.82
  404.3 0.6 broadcast_multiply_fusion
  404.9 78.1 %reduce-scatter.13.cloned.1.call-done = bf16[160,80]{1,0:T(8,128)(2,1)} async-done(((bf16[2560,80]{1,0:T(8,128)(2,1)}), bf16[160,80]{1,0:T(8,128)(2,1)}) %reduce-scatter.13.cloned.1.call-update) | async-done | bytes 25616
  483.0 0.9 copy.81
  483.9 0.6 multiply_convert_fusion.4
  484.5 80.1 %reduce-scatter.15.cloned.1.call-done = bf16[80,160]{1,0:T(8,128)(2,1)} async-done(((bf16[1280,160]{1,0:T(8,128)(2,1)}), bf16[80,160]{1,0:T(8,128)(2,1)}) %reduce-scatter.15.cloned.1.call-update) | async-done | bytes 25616
  564.6 0.9 copy.83
  565.5 0.6 multiply_convert_fusion.3
  (79 shorter events, 4.4 us)
Async XLA Ops:
  7.2 14.3 %copy-start = (bf16[1,192,1280]{2,1,0:T(8,128)(2,1)S(1)}, bf16[1,192,1280]{2,1,0:T(8,128)(2,1)}, u32[]{:S(2)}) copy-start(bf16[1,192,1280]{2,1,0:T(8,128)(2,1)} %param.14) | copy-start | bytes 1474564
  7.2 75.9 %all-gather.8.cloned.1.call-start = ((), (), s32[]{:S(2)}) async-start(), calls=%async_computation.7 | async-start | bytes 6963200 | tf_op jit(solution)/shard_map/all_gather | solution.py:39
  7.9 143.1 %all-gather.6.cloned.1.call-start = ((), (), s32[]{:S(2)}) async-start(), calls=%async_computation.6 | async-start | bytes 6963200 | tf_op jit(solution)/shard_map/all_gather | solution.py:40
  12.9 16.1 %all-to-all-start = ((s32[16,1,32]{2,1,0:T(1,128)}), s32[16,1,32]{2,1,0:T(1,128)S(1)}, u32[]{:S(2)}, u32[]{:S(2)}) async-start(s32[16,1,32]{2,1,0:T(1,128)} %all_to_all.9), calls=%async_computation | async-start | bytes 16384 | tf_op jit(solution)/shard_map/all_to_all | solution.py:67
  29.0 4.6 copy-start.8
  29.0 4.8 copy-start.9
  29.0 50.4 %all-to-all-start.1 = ((bf16[16,32,1280]{2,1,0:T(8,128)(2,1)}), bf16[16,32,1280]{2,1,0:T(8,128)(2,1)}, u32[]{:S(2)}, u32[]{:S(2)}) async-start(bf16[16,32,1280]{2,1,0:T(8,128)(2,1)} %bitcast.13), calls=%async_computation.1 | async-start | bytes 2621440 | tf_op jit(solution)/shard_map/all_to_all | solution.py:60
  33.5 1.0 copy-start.10
  33.5 1.2 copy-start.14
  33.6 194.7 %reduce-scatter.9.cloned.1.call-start = ((), (), s32[]{:S(2)}) async-start(), calls=%async_computation.8 | async-start | bytes 6963200 | tf_op jit(solution)/shard_map/reduce_scatter | solution.py:132
  33.8 1.7 copy-start.3
  34.5 1.1 copy-start.11
  34.7 0.9 copy-start.1
  35.6 1.0 copy-start.17
  36.9 0.7 copy-start.6
  37.7 0.7 copy-start.16
  37.7 1.9 copy-start.15
  37.7 40.0 %copy-start.13 = (bf16[1,128,1280]{2,1,0:T(8,128)(2,1)S(1)}, bf16[1,128,1280]{2,1,0:T(8,128)(2,1)}, u32[]{:S(2)}) copy-start(bf16[1,128,1280]{2,1,0:T(8,128)(2,1)} %param.13) | copy-start | bytes 983044
  160.8 136.0 %reduce-scatter.11.cloned.1.call-start = ((), (), s32[]{:S(2)}) async-start(), calls=%async_computation.9 | async-start | bytes 6963200 | tf_op jit(solution)/shard_map/reduce_scatter | solution.py:135
  165.5 236.7 %all-gather.10.cloned.1.call-start = ((), (), s32[]{:S(2)}) async-start(), calls=%async_computation.10 | async-start | bytes 1315840 | tf_op jit(solution)/shard_map/all_gather | solution.py:148
  171.3 311.7 %reduce-scatter.13.cloned.1.call-start = ((), (), s32[]{:S(2)}) async-start(), calls=%async_computation.11 | async-start | bytes 696320
  230.4 334.2 %reduce-scatter.15.cloned.1.call-start = ((), (), s32[]{:S(2)}) async-start(), calls=%async_computation.12 | async-start | bytes 696320
  230.5 1.0 copy-start.7
  230.8 2.8 copy-start.5
  230.8 1.1 copy-start.12
  232.0 1.7 copy-start.4
  233.6 65.2 %copy-start.2 = (bf16[1,128,1280]{1,2,0:T(8,128)(2,1)S(1)}, bf16[1,128,1280]{1,2,0:T(8,128)(2,1)}, u32[]{:S(2)}) copy-start(bf16[1,128,1280]{1,2,0:T(8,128)(2,1)} %copy-done.1) | copy-start | bytes 983044
  298.9 2.3 copy-start.18
Sparse Core Ops, SparseCore 0:
  10.4 70.4 all-gather.7
  83.3 67.5 all-gather.5
  160.9 67.3 reduce-scatter.8
  230.7 65.9 reduce-scatter.10
  300.7 101.4 all-gather.9
  405.6 77.4 reduce-scatter.12
  486.5 78.0 reduce-scatter.14
